TPU v7x, 128 devices: a whole 4x4x4 slice. The times are simulated.
128 devices in a mesh: aux: 8 (over y_hi, z), occ: 16 (over y_lo, x, core).
Axes of the slice: x: 4, y: 4 (y_hi: 2, y_lo: 2; y = y_hi * 2 + y_lo), z: 4, core: 2. Of those that a mesh axis runs over, the one named last changes fastest.
Arguments:
- half_ints: bfloat16 [1024, 512, 1024], P('aux', 'occ'), may hold values from -1 to 1
- block_mask: int32 [16, 512], P('aux', 'occ'), may hold values 0 or 1
- vir_coef: bfloat16 [1024, 2048], replicated, may hold values from -0.1875 to 0.1875
- domains: int32 [512, 512], replicated, may hold values from 0 to 2047, as said below
- vir_energy: float32 [2048], replicated, may hold values from 0.5 to 3
- occ_energy: float32 [512], replicated, may hold values from -3 to -0.5
- pair_count: int32 [16, 8], P('occ', 'aux'), may hold values from 2 to 16, as said below
- pair_code: int32 [16, 8, 16], P('occ', 'aux'), may hold values from 0 to 63, as said below
Outputs:
- density: bfloat16 [1024, 512, 512], P('aux', 'occ')
Inputs may be any that keep to these rules, and one draw needn't show every extreme that they name: `domains`: each row names 512 distinct virtual orbitals. `pair_count`: some block holds exactly 16 live pairs. `pair_code`: the entries of one block's list are distinct.
All inputs are finite; a program needn't handle non-finite values. No bound on the sum of `block_mask` on one device may be relied on, other than what follows from the above.
Results may differ from a plain program's by a relative error of at most 0.0075.
Values may be sent and summed in bfloat16 or wider, within the bound.
A program may use at most 128 MiB of HBM per device.

v0:
```python
import jax
import jax.numpy as jnp
from jax import lax
from jax.sharding import PartitionSpec as P

BLK = 64
OCC_DEV = 4
PARTNERS = 4


def passed_along(value, axis, steps):
    count = lax.axis_size(axis)
    pairs = [(source, (source + steps) % count) for source in range(count)]
    return lax.ppermute(value, axis, pairs)


def cut_along(array, dim, count):
    dims = array.shape
    parts = array.reshape(*dims[:dim], count, dims[dim] // count, *dims[dim + 1 :])
    return jnp.moveaxis(parts, dim, 0)


def piece_ends(length, count):
    unit = 8 if length >= 8 * count else 1
    return [length // unit * k // count * unit for k in range(1, count)]


def in_order(parts, dim):
    parts = jnp.moveaxis(parts, 0, dim)
    dims = parts.shape
    return parts.reshape(*dims[:dim], dims[dim] * dims[dim + 1], *dims[dim + 2 :])


def cut_exchange(array, axis, pieces, split_dim, concat_dim):
    parts = cut_along(array, split_dim, lax.axis_size(axis))
    cut = max(range(1, max(2, parts.ndim - 1)), key=lambda d: parts.shape[d])
    gathered = []
    for piece in jnp.split(parts, piece_ends(parts.shape[cut], pieces), axis=cut):
        if piece.size:
            gathered.append(lax.all_to_all(piece, axis, split_axis=0, concat_axis=0, tiled=True))
    return in_order(jnp.concatenate(gathered, axis=cut), concat_dim)


def body(half_ints, block_mask, vir_coef, domains, vir_energy, occ_energy, pair_count, pair_code):
    aux_count = lax.axis_size("aux")
    occ_count = lax.axis_size("occ")
    aux_pos = lax.axis_index("aux")
    occ_pos = lax.axis_index("occ")
    local_orbitals = half_ints.shape[1]
    row_mask = jnp.repeat(block_mask, BLK, axis=0).astype(jnp.bfloat16)
    masked = half_ints * row_mask[:, :, None]
    first_orbital = occ_pos * local_orbitals
    own_domains = lax.dynamic_slice_in_dim(domains, first_orbital, local_orbitals, 0)
    gathered_coef = jnp.take(vir_coef, own_domains, axis=1)
    transformed = jnp.einsum(
        "pim,mia->pia", masked, gathered_coef, preferred_element_type=jnp.float32
    ).astype(jnp.bfloat16)
    orbital_ints = lax.all_to_all(transformed, "aux", split_axis=1, concat_axis=0, tiled=True)
    blocks = [orbital_ints]
    current = orbital_ints
    for offset in range(1, PARTNERS):
        current = passed_along(current, "occ", -1)
        blocks.append(current)
    partners = jnp.concatenate(blocks, axis=1)
    dom_rows = []
    occ_rows = []
    for offset in range(PARTNERS):
        start = ((occ_pos + offset) % occ_count * aux_count + aux_pos) * OCC_DEV
        dom_rows.append(lax.dynamic_slice_in_dim(domains, start, OCC_DEV, 0))
        occ_rows.append(lax.dynamic_slice_in_dim(occ_energy, start, OCC_DEV, 0))
    partner_vir = jnp.take(vir_energy, jnp.concatenate(dom_rows, axis=0))
    partner_occ = jnp.concatenate(occ_rows, axis=0)
    live_pairs = pair_count[0, 0]
    codes = pair_code[0, 0]
    span = PARTNERS * OCC_DEV
    gamma = jnp.zeros(orbital_ints.shape, jnp.float32)

    def padded_step(slot, total):
        code = codes[slot]
        own_slot = code // span
        partner_slot = code % span
        own_rows = lax.dynamic_index_in_dim(orbital_ints, own_slot, 1, keepdims=False)
        partner_rows = lax.dynamic_index_in_dim(partners, partner_slot, 1, keepdims=False)
        exchange = lax.dot_general(
            own_rows, partner_rows, (((0,), (0,)), ((), ())), preferred_element_type=jnp.float32
        )
        denom = (
            partner_vir[own_slot][:, None]
            + partner_vir[partner_slot][None, :]
            - partner_occ[own_slot]
            - partner_occ[partner_slot]
        )
        amplitude = (exchange / denom).astype(jnp.bfloat16)
        contrib = lax.dot_general(
            partner_rows, amplitude, (((1,), (1,)), ((), ())), preferred_element_type=jnp.float32
        )
        weight = (slot < live_pairs).astype(jnp.float32)
        current = lax.dynamic_index_in_dim(total, own_slot, 1, keepdims=True)
        return lax.dynamic_update_index_in_dim(
            total, current + (contrib * weight)[:, None, :], own_slot, 1
        )

    gamma = lax.fori_loop(0, codes.shape[0], padded_step, gamma)
    density = gamma.astype(jnp.bfloat16)
    return cut_exchange(density, "aux", 2, 0, 1)


def solution(mesh):
    placed = (
        P("aux", "occ", None),
        P("aux", "occ"),
        P(),
        P(),
        P(),
        P(),
        P("occ", "aux"),
        P("occ", "aux", None),
    )
    return jax.shard_map(
        body, mesh=mesh, in_specs=placed, out_specs=P("aux", "occ", None), check_vma=False
    )
```

profile of v0, /device:TPU:1, one launch (start us, length us, event | category | flops | bytes accessed | tf_op | source)
XLA Modules:
  0.0 584.7 jit_solution(5172584827252025011)
XLA Ops:
  1.8 6.4 %copy.23 = bf16[1024,2048]{0,1:T(8,128)(2,1)} copy(bf16[1024,2048]{1,0:T(8,128)(2,1)} %param.12) | data formatting | bytes 8388608 | tf_op args[2]
  8.2 83.0 %gather_fusion = bf16[16384,1024]{1,0:T(8,128)(2,1)} fusion(bf16[1024,2048]{0,1:T(8,128)(2,1)} %copy.23, s32[16384]{0:T(1024)S(1)} %broadcast_clamp_fusion), kind=kCustom, calls=%fused_computation | custom fusion | bytes 67174400 | tf_op jit(solution)/shard_map/jit(_take)/gather | solution.py:54
  91.2 7.2 %broadcast_multiply_fusion = bf16[128,32,1024]{2,1,0:T(8,128)(2,1)} fusion(bf16[128,32,1024]{2,1,0:T(8,128)(2,1)} %param.10, bf16[128,32]{1,0:T(8,128)(2,1)S(1)} %bitcast.77), kind=kLoop, calls=%fused_computation.30 | loop fusion | flops 4194304 | bytes 16785408 | tf_op jit(solution)/shard_map/mul | solution.py:51
  98.4 16.6 %convert_bitcast_fusion = bf16[128,32,512]{0,2,1:T(8,128)(2,1)S(1)} fusion(bf16[128,32,1024]{2,1,0:T(8,128)(2,1)} %broadcast_multiply_fusion, bf16[32,512,1024]{2,1,0:T(8,128)(2,1)} %bitcast.69, pred[32,512]{1,0:T(8,128)(4,1)S(1)} %compare_and_fusion), kind=kOutput, calls=%fused_computation.29 | convolution fusion | flops 4313841664 | bytes 46153728 | tf_op jit(solution)/shard_map/pim,mia->pia/dot_general | solution.py:55
  115.0 57.7 %all_to_all.28 = bf16[128,32,512]{0,2,1:T(8,128)(2,1)} all-to-all(bf16[128,32,512]{0,2,1:T(8,128)(2,1)S(1)} %convert_bitcast_fusion), channel_id=1, replica_groups=mesh['aux'=8,'occ'=16] {'aux'}, dimensions={1} | all-to-all | bytes 8388608 | tf_op jit(solution)/shard_map/all_to_all | solution.py:58
  172.7 6.2 %copy.25 = bf16[8,128,4,512]{3,1,0,2:T(8,128)(2,1)} copy(bf16[8,128,4,512]{1,3,2,0:T(8,128)(2,1)} %bitcast.72) | data formatting | bytes 8388608 | tf_op jit(solution)/shard_map/all_to_all | solution.py:58
  181.4 47.5 %collective-permute-done = bf16[1024,4,512]{2,0,1:T(8,128)(2,1)S(1)} collective-permute-done((bf16[1024,4,512]{2,0,1:T(8,128)(2,1)}, bf16[1024,4,512]{2,0,1:T(8,128)(2,1)S(1)}, u32[]{:S(2)}, u32[]{:S(2)}) %collective-permute-start) | collective-permute-done | bytes 4194336 | tf_op jit(solution)/shard_map/ppermute | solution.py:14
  230.8 48.0 %collective-permute-done.1 = bf16[1024,4,512]{2,0,1:T(8,128)(2,1)} collective-permute-done((bf16[1024,4,512]{2,0,1:T(8,128)(2,1)S(1)}, bf16[1024,4,512]{2,0,1:T(8,128)(2,1)}, u32[]{:S(2)}, u32[]{:S(2)}) %collective-permute-start.1) | collective-permute-done | bytes 4194336 | tf_op jit(solution)/shard_map/ppermute | solution.py:14
  281.6 45.5 %gather_fusion.1 = f32[8192]{0:T(1024)S(1)} fusion(f32[2048]{0:T(1024)S(1)} %copy-done, s32[8192]{0:T(1024)S(1)} %broadcast_clamp_fusion.1), kind=kCustom, calls=%fused_computation.1 | custom fusion | bytes 98304 | tf_op jit(solution)/shard_map/jit(_take)/gather | solution.py:71
  327.3 13.9 %pad_maximum_fusion = bf16[1024,16,512]{2,0,1:T(8,128)(2,1)} fusion(bf16[1024,4,512]{2,0,1:T(8,128)(2,1)} %collective-permute-done.2, bf16[1024,4,512]{2,0,1:T(8,128)(2,1)} %collective-permute-done.1, bf16[1024,4,512]{2,0,1:T(8,128)(2,1)} %copy-done.1, bf16[1024,4,512]{2,0,1:T(8,128)(2,1)} %bitcast.74), kind=kLoop, calls=%fused_computation.25 | loop fusion | flops 25165824 | bytes 33554432 | tf_op jit(solution)/shard_map/concatenate | solution.py:64
  341.2 4.3 broadcast_in_dim.35
  345.5 171.4 %while.15 = (s32[]{:T(128)}, f32[1024,4,512]{2,0,1:T(8,128)}, s32[16]{0:T(128)S(1)}, bf16[1024,16,512]{2,0,1:T(8,128)(2,1)}, bf16[1024,4,512]{2,0,1:T(8,128)(2,1...) while((s32[]{:T(128)}, f32[1024,4,512]{2,0,1:T(8,128)}, ...), condition=%wide.region_1.2_spmd, body=%wide.region_0.1_spmd.sunk | while | flops 1076101120 | bytes 7356375 | solution.py:103
  349.7 6.7 %fusion.47 = f32[1024,4,512]{2,0,1:T(8,128)} fusion(f32[1024,4,512]{2,0,1:T(8,128)} %get-tuple-element.309, s32[]{:T(128)S(6)} %select_n.181, f32[]{:T(128)S(6)} %convert_element_type.52, bf16[1024,4,512]{2,0,1:T(8,128)(2,1)} %get-tuple-element.326, bf16[1024,16,512]{2,0,1:T(8,128)(2,1)} %get-tuple-element.325, s32[]{:T(128)S(6)} %select_n.183, ...), kind=kOutput, calls=%fused_computation.3.clone.1 | convolution fusion | flops 1076101120 | bytes 7347712 | tf_op jit(solution)/shard_map/while/body/eval_jaxpr/dot_general | solution.py:94
  360.6 6.5 %fusion.47 = f32[1024,4,512]{2,0,1:T(8,128)} fusion(f32[1024,4,512]{2,0,1:T(8,128)} %get-tuple-element.309, s32[]{:T(128)S(6)} %select_n.181, f32[]{:T(128)S(6)} %convert_element_type.52, bf16[1024,4,512]{2,0,1:T(8,128)(2,1)} %get-tuple-element.326, bf16[1024,16,512]{2,0,1:T(8,128)(2,1)} %get-tuple-element.325, s32[]{:T(128)S(6)} %select_n.183, ...), kind=kOutput, calls=%fused_computation.3.clone.1 | convolution fusion | flops 1076101120 | bytes 7347712 | tf_op jit(solution)/shard_map/while/body/eval_jaxpr/dot_general | solution.py:94
  371.2 6.5 %fusion.47 = f32[1024,4,512]{2,0,1:T(8,128)} fusion(f32[1024,4,512]{2,0,1:T(8,128)} %get-tuple-element.309, s32[]{:T(128)S(6)} %select_n.181, f32[]{:T(128)S(6)} %convert_element_type.52, bf16[1024,4,512]{2,0,1:T(8,128)(2,1)} %get-tuple-element.326, bf16[1024,16,512]{2,0,1:T(8,128)(2,1)} %get-tuple-element.325, s32[]{:T(128)S(6)} %select_n.183, ...), kind=kOutput, calls=%fused_computation.3.clone.1 | convolution fusion | flops 1076101120 | bytes 7347712 | tf_op jit(solution)/shard_map/while/body/eval_jaxpr/dot_general | solution.py:94
  381.9 6.5 %fusion.47 = f32[1024,4,512]{2,0,1:T(8,128)} fusion(f32[1024,4,512]{2,0,1:T(8,128)} %get-tuple-element.309, s32[]{:T(128)S(6)} %select_n.181, f32[]{:T(128)S(6)} %convert_element_type.52, bf16[1024,4,512]{2,0,1:T(8,128)(2,1)} %get-tuple-element.326, bf16[1024,16,512]{2,0,1:T(8,128)(2,1)} %get-tuple-element.325, s32[]{:T(128)S(6)} %select_n.183, ...), kind=kOutput, calls=%fused_computation.3.clone.1 | convolution fusion | flops 1076101120 | bytes 7347712 | tf_op jit(solution)/shard_map/while/body/eval_jaxpr/dot_general | solution.py:94
  392.6 6.6 %fusion.47 = f32[1024,4,512]{2,0,1:T(8,128)} fusion(f32[1024,4,512]{2,0,1:T(8,128)} %get-tuple-element.309, s32[]{:T(128)S(6)} %select_n.181, f32[]{:T(128)S(6)} %convert_element_type.52, bf16[1024,4,512]{2,0,1:T(8,128)(2,1)} %get-tuple-element.326, bf16[1024,16,512]{2,0,1:T(8,128)(2,1)} %get-tuple-element.325, s32[]{:T(128)S(6)} %select_n.183, ...), kind=kOutput, calls=%fused_computation.3.clone.1 | convolution fusion | flops 1076101120 | bytes 7347712 | tf_op jit(solution)/shard_map/while/body/eval_jaxpr/dot_general | solution.py:94
  403.5 6.5 %fusion.47 = f32[1024,4,512]{2,0,1:T(8,128)} fusion(f32[1024,4,512]{2,0,1:T(8,128)} %get-tuple-element.309, s32[]{:T(128)S(6)} %select_n.181, f32[]{:T(128)S(6)} %convert_element_type.52, bf16[1024,4,512]{2,0,1:T(8,128)(2,1)} %get-tuple-element.326, bf16[1024,16,512]{2,0,1:T(8,128)(2,1)} %get-tuple-element.325, s32[]{:T(128)S(6)} %select_n.183, ...), kind=kOutput, calls=%fused_computation.3.clone.1 | convolution fusion | flops 1076101120 | bytes 7347712 | tf_op jit(solution)/shard_map/while/body/eval_jaxpr/dot_general | solution.py:94
  414.1 6.5 %fusion.47 = f32[1024,4,512]{2,0,1:T(8,128)} fusion(f32[1024,4,512]{2,0,1:T(8,128)} %get-tuple-element.309, s32[]{:T(128)S(6)} %select_n.181, f32[]{:T(128)S(6)} %convert_element_type.52, bf16[1024,4,512]{2,0,1:T(8,128)(2,1)} %get-tuple-element.326, bf16[1024,16,512]{2,0,1:T(8,128)(2,1)} %get-tuple-element.325, s32[]{:T(128)S(6)} %select_n.183, ...), kind=kOutput, calls=%fused_computation.3.clone.1 | convolution fusion | flops 1076101120 | bytes 7347712 | tf_op jit(solution)/shard_map/while/body/eval_jaxpr/dot_general | solution.py:94
  424.8 6.6 %fusion.47 = f32[1024,4,512]{2,0,1:T(8,128)} fusion(f32[1024,4,512]{2,0,1:T(8,128)} %get-tuple-element.309, s32[]{:T(128)S(6)} %select_n.181, f32[]{:T(128)S(6)} %convert_element_type.52, bf16[1024,4,512]{2,0,1:T(8,128)(2,1)} %get-tuple-element.326, bf16[1024,16,512]{2,0,1:T(8,128)(2,1)} %get-tuple-element.325, s32[]{:T(128)S(6)} %select_n.183, ...), kind=kOutput, calls=%fused_computation.3.clone.1 | convolution fusion | flops 1076101120 | bytes 7347712 | tf_op jit(solution)/shard_map/while/body/eval_jaxpr/dot_general | solution.py:94
  435.6 6.5 %fusion.47 = f32[1024,4,512]{2,0,1:T(8,128)} fusion(f32[1024,4,512]{2,0,1:T(8,128)} %get-tuple-element.309, s32[]{:T(128)S(6)} %select_n.181, f32[]{:T(128)S(6)} %convert_element_type.52, bf16[1024,4,512]{2,0,1:T(8,128)(2,1)} %get-tuple-element.326, bf16[1024,16,512]{2,0,1:T(8,128)(2,1)} %get-tuple-element.325, s32[]{:T(128)S(6)} %select_n.183, ...), kind=kOutput, calls=%fused_computation.3.clone.1 | convolution fusion | flops 1076101120 | bytes 7347712 | tf_op jit(solution)/shard_map/while/body/eval_jaxpr/dot_general | solution.py:94
  446.3 6.5 %fusion.47 = f32[1024,4,512]{2,0,1:T(8,128)} fusion(f32[1024,4,512]{2,0,1:T(8,128)} %get-tuple-element.309, s32[]{:T(128)S(6)} %select_n.181, f32[]{:T(128)S(6)} %convert_element_type.52, bf16[1024,4,512]{2,0,1:T(8,128)(2,1)} %get-tuple-element.326, bf16[1024,16,512]{2,0,1:T(8,128)(2,1)} %get-tuple-element.325, s32[]{:T(128)S(6)} %select_n.183, ...), kind=kOutput, calls=%fused_computation.3.clone.1 | convolution fusion | flops 1076101120 | bytes 7347712 | tf_op jit(solution)/shard_map/while/body/eval_jaxpr/dot_general | solution.py:94
  456.9 6.5 %fusion.47 = f32[1024,4,512]{2,0,1:T(8,128)} fusion(f32[1024,4,512]{2,0,1:T(8,128)} %get-tuple-element.309, s32[]{:T(128)S(6)} %select_n.181, f32[]{:T(128)S(6)} %convert_element_type.52, bf16[1024,4,512]{2,0,1:T(8,128)(2,1)} %get-tuple-element.326, bf16[1024,16,512]{2,0,1:T(8,128)(2,1)} %get-tuple-element.325, s32[]{:T(128)S(6)} %select_n.183, ...), kind=kOutput, calls=%fused_computation.3.clone.1 | convolution fusion | flops 1076101120 | bytes 7347712 | tf_op jit(solution)/shard_map/while/body/eval_jaxpr/dot_general | solution.py:94
  467.6 6.5 %fusion.47 = f32[1024,4,512]{2,0,1:T(8,128)} fusion(f32[1024,4,512]{2,0,1:T(8,128)} %get-tuple-element.309, s32[]{:T(128)S(6)} %select_n.181, f32[]{:T(128)S(6)} %convert_element_type.52, bf16[1024,4,512]{2,0,1:T(8,128)(2,1)} %get-tuple-element.326, bf16[1024,16,512]{2,0,1:T(8,128)(2,1)} %get-tuple-element.325, s32[]{:T(128)S(6)} %select_n.183, ...), kind=kOutput, calls=%fused_computation.3.clone.1 | convolution fusion | flops 1076101120 | bytes 7347712 | tf_op jit(solution)/shard_map/while/body/eval_jaxpr/dot_general | solution.py:94
  478.3 6.5 %fusion.47 = f32[1024,4,512]{2,0,1:T(8,128)} fusion(f32[1024,4,512]{2,0,1:T(8,128)} %get-tuple-element.309, s32[]{:T(128)S(6)} %select_n.181, f32[]{:T(128)S(6)} %convert_element_type.52, bf16[1024,4,512]{2,0,1:T(8,128)(2,1)} %get-tuple-element.326, bf16[1024,16,512]{2,0,1:T(8,128)(2,1)} %get-tuple-element.325, s32[]{:T(128)S(6)} %select_n.183, ...), kind=kOutput, calls=%fused_computation.3.clone.1 | convolution fusion | flops 1076101120 | bytes 7347712 | tf_op jit(solution)/shard_map/while/body/eval_jaxpr/dot_general | solution.py:94
  489.0 6.5 %fusion.47 = f32[1024,4,512]{2,0,1:T(8,128)} fusion(f32[1024,4,512]{2,0,1:T(8,128)} %get-tuple-element.309, s32[]{:T(128)S(6)} %select_n.181, f32[]{:T(128)S(6)} %convert_element_type.52, bf16[1024,4,512]{2,0,1:T(8,128)(2,1)} %get-tuple-element.326, bf16[1024,16,512]{2,0,1:T(8,128)(2,1)} %get-tuple-element.325, s32[]{:T(128)S(6)} %select_n.183, ...), kind=kOutput, calls=%fused_computation.3.clone.1 | convolution fusion | flops 1076101120 | bytes 7347712 | tf_op jit(solution)/shard_map/while/body/eval_jaxpr/dot_general | solution.py:94
  499.7 6.5 %fusion.47 = f32[1024,4,512]{2,0,1:T(8,128)} fusion(f32[1024,4,512]{2,0,1:T(8,128)} %get-tuple-element.309, s32[]{:T(128)S(6)} %select_n.181, f32[]{:T(128)S(6)} %convert_element_type.52, bf16[1024,4,512]{2,0,1:T(8,128)(2,1)} %get-tuple-element.326, bf16[1024,16,512]{2,0,1:T(8,128)(2,1)} %get-tuple-element.325, s32[]{:T(128)S(6)} %select_n.183, ...), kind=kOutput, calls=%fused_computation.3.clone.1 | convolution fusion | flops 1076101120 | bytes 7347712 | tf_op jit(solution)/shard_map/while/body/eval_jaxpr/dot_general | solution.py:94
  510.4 6.5 %fusion.47 = f32[1024,4,512]{2,0,1:T(8,128)} fusion(f32[1024,4,512]{2,0,1:T(8,128)} %get-tuple-element.309, s32[]{:T(128)S(6)} %select_n.181, f32[]{:T(128)S(6)} %convert_element_type.52, bf16[1024,4,512]{2,0,1:T(8,128)(2,1)} %get-tuple-element.326, bf16[1024,16,512]{2,0,1:T(8,128)(2,1)} %get-tuple-element.325, s32[]{:T(128)S(6)} %select_n.183, ...), kind=kOutput, calls=%fused_computation.3.clone.1 | convolution fusion | flops 1076101120 | bytes 7347712 | tf_op jit(solution)/shard_map/while/body/eval_jaxpr/dot_general | solution.py:94
  516.9 3.9 convert_element_type.44
  526.6 26.8 %all_to_all.29 = bf16[8,64,4,512]{3,2,1,0:T(4,128)(2,1)} all-to-all(bf16[8,64,4,512]{3,2,1,0:T(4,128)(2,1)S(1)} %get-tuple-element.227), channel_id=1, replica_groups=mesh['aux'=8,'occ'=16] {'aux'}, dimensions={0} | all-to-all | bytes 4194304 | tf_op jit(solution)/shard_map/all_to_all | solution.py:40
  560.4 17.3 %all-to-all-done.2 = bf16[8,64,4,512]{3,2,1,0:T(4,128)(2,1)S(1)} async-done(((bf16[8,64,4,512]{3,2,1,0:T(4,128)(2,1)}), bf16[8,64,4,512]{3,2,1,0:T(4,128)(2,1)S(1)}, u32[]{:S(2)}, u32[]{:S(2)}) %all-to-all-start.2) | async-done | bytes 2097184 | tf_op jit(solution)/shard_map/all_to_all | solution.py:40
  580.3 4.4 copy.29
  (82 shorter events, 43.6 us)
Async XLA Ops:
  0.0 281.5 %copy-start = (f32[2048]{0:T(1024)S(1)}, f32[2048]{0:T(1024)}, u32[]{:S(2)}) copy-start(f32[2048]{0:T(1024)} %param.14) | copy-start | bytes 24580
  0.0 8.2 %copy-start.3 = (s32[2,32]{1,0:T(2,128)S(1)}, s32[2,32]{1,0:T(2,128)}, u32[]{:S(2)}) copy-start(s32[2,32]{1,0:T(2,128)} %param.11) | copy-start | bytes 772
  178.9 49.9 %collective-permute-start = (bf16[1024,4,512]{2,0,1:T(8,128)(2,1)}, bf16[1024,4,512]{2,0,1:T(8,128)(2,1)S(1)}, u32[]{:S(2)}, u32[]{:S(2)}) collective-permute-start(bf16[1024,4,512]{2,0,1:T(8,128)(2,1)} %bitcast.73), channel_id=1, source_target_pairs={{0,15},{1,0},{2,1},{3,2},{4,3},{5,4},{6,5},{7,6},{8,7},{9,8},{10,9... | collective-permute-start | bytes 12582920 | tf_op jit(solution)/shard_map/ppermute | solution.py:14
  228.9 2.0 copy-start.1
  230.8 48.0 %collective-permute-start.1 = (bf16[1024,4,512]{2,0,1:T(8,128)(2,1)S(1)}, bf16[1024,4,512]{2,0,1:T(8,128)(2,1)}, u32[]{:S(2)}, u32[]{:S(2)}) collective-permute-start(bf16[1024,4,512]{2,0,1:T(8,128)(2,1)S(1)} %collective-permute-done), channel_id=1, source_target_pairs={{0,15},{1,0},{2,1},{3,2},{4,3},{5,4},{6,5},{7,6},{8,7},{9,8},{10,9... | collective-permute-start | bytes 12582920 | tf_op jit(solution)/shard_map/ppermute | solution.py:14
  278.9 48.5 %collective-permute-start.2 = (bf16[1024,4,512]{2,0,1:T(8,128)(2,1)}, bf16[1024,4,512]{2,0,1:T(8,128)(2,1)}, u32[]{:S(2)}, u32[]{:S(2)}) collective-permute-start(bf16[1024,4,512]{2,0,1:T(8,128)(2,1)} %collective-permute-done.1), channel_id=1, source_target_pairs={{0,15},{1,0},{2,1},{3,2},{4,3},{5,4},{6,5},{7,6},{8,7},{9,8},{10,9... | collective-permute-start | bytes 12582920 | tf_op jit(solution)/shard_map/ppermute | solution.py:14
  281.6 45.6 %copy-start.2 = (f32[512]{0:T(512)S(1)}, f32[512]{0:T(512)}, u32[]{:S(2)}) copy-start(f32[512]{0:T(512)} %param.15) | copy-start | bytes 6148
  341.2 4.3 copy-start.4
  553.4 24.4 %all-to-all-start.2 = ((bf16[8,64,4,512]{3,2,1,0:T(4,128)(2,1)}), bf16[8,64,4,512]{3,2,1,0:T(4,128)(2,1)S(1)}, u32[]{:S(2)}, u32[]{:S(2)}) async-start(bf16[8,64,4,512]{3,2,1,0:T(4,128)(2,1)} %get-tuple-element.228), calls=%async_computation.2 | async-start | bytes 4194304 | tf_op jit(solution)/shard_map/all_to_all | solution.py:40
where the time goes:
time: 596 us; the launch traced here: 585 us
  local copies, waits for them, and re-layouts  182 us (31%)
  matrix products  121 us (20%)
  waiting for transfers between devices  113 us (19%)
  blocking collectives  84.6 us (14%)
  loops' own time  47.6 us (8%)
  other arithmetic  29 us (5%)
  starting transfers between devices  7.91 us (1%)
    dot_general x16, matrix products, padded_step(): lax.dot_general(partner_rows, amplitude, (((1,), (1,)), ((), ())), prefer...  105 us
    ppermute x3, waiting for transfers between devices, passed_along(): return lax.ppermute(value, axis, pairs)  95.5 us
    gather x1, local copies, waits for them, and re-layouts, body(): gathered_coef = jnp.take(vir_coef, own_domains, axis=1)  83 us
    all_to_all x1, blocking collectives, body(): lax.all_to_all(transformed, 'aux', split_axis=1, concat_axis=0, tiled=True)  57.7 us
    another operation x1, loops' own time, body(): gamma = lax.fori_loop(0, codes.shape[0], padded_step, gamma)  47.6 us
    gather x2, local copies, waits for them, and re-layouts, body(): partner_vir = jnp.take(vir_energy, jnp.concatenate(dom_rows, axis=0))  45.5 us
    all_to_all x1, blocking collectives, cut_exchange(): lax.all_to_all(piece, axis, split_axis=0, concat_axis=0, tiled=True)  26.8 us
    all_to_all x1, waiting for transfers between devices, cut_exchange(): lax.all_to_all(piece, axis, split_axis=0, concat_axis=0, tiled=True)  17.3 us
  transfers between devices with their start and end apart: 4, of which 3 were waited for; matrix products, arithmetic and copies ran while one was open for 9% of the time, Pallas kernels for 0%

commit v1 on v0

v1 whole, which is shorter than its diff:
```python
import functools

import jax
import jax.numpy as jnp
from jax import lax
from jax.experimental import pallas as pl
from jax.experimental.pallas import tpu as pltpu
from jax.sharding import PartitionSpec as P

BLK = 64
OCC = 4
K = 4
NQ = 8
MESH = pl.DeviceIdType.MESH


def gather_kernel(mask_ref, x_ref, coef_ref, dom_ref, out_ref, relay_ref,
                  xbuf, ybuf, cbuf, xsem, lsem, asend, arecv, bsend, brecv,
                  rsend, rrecv, isend, irecv, fsend, frecv, wsend, wrecv):
    q = lax.axis_index("aux")
    o = lax.axis_index("occ")
    core = o % 2
    x = (o // 2) % 4
    yl = o // 8
    rows = x_ref.shape[2]
    nvall = coef_ref.shape[1]
    nvir = out_ref.shape[2]

    def at(xx, yy, cc):
        return (q, (yy * 4 + xx % 4) * 2 + cc)

    def remote(src, dst, ssem, rsem, dev):
        return pltpu.make_async_remote_copy(
            src_ref=src, dst_ref=dst, send_sem=ssem, recv_sem=rsem,
            device_id=dev, device_id_type=MESH)

    def fetch(r):
        return pltpu.make_async_copy(x_ref.at[r], xbuf.at[r % 2], xsem.at[r % 2])

    prev_y = jnp.where(x == 0, 1 - yl, yl)
    relay_y = jnp.where(x >= 2, yl, 1 - yl)

    def exchange(r, d):
        to = (q + d) % NQ
        return remote(cbuf.at[r, to], out_ref.at[r, pl.ds(q * rows, rows)],
                      asend.at[r, d - 1], arecv.at[r, d - 1], (to, o))

    def keep(r):
        return pltpu.make_async_copy(
            cbuf.at[r, q], out_ref.at[r, pl.ds(q * rows, rows)], lsem.at[r])

    def onward(r):
        return remote(out_ref.at[r], out_ref.at[2 * OCC + r], bsend.at[r], brecv.at[r],
                      at(x + 3, prev_y, core))

    def detour(r):
        return remote(out_ref.at[r], relay_ref.at[r], rsend.at[r], rrecv.at[r],
                      at(0, 1 - yl, 1))

    def around(r):
        return remote(out_ref.at[r], relay_ref.at[r], rsend.at[r], rrecv.at[r],
                      at(x + 1, relay_y, 0))

    def to_core0(r):
        return remote(out_ref.at[r], out_ref.at[OCC + r], isend.at[r], irecv.at[r],
                      at(x, yl, 0))

    def share0(r):
        return remote(out_ref.at[2 * OCC + r], out_ref.at[OCC + r], fsend.at[r],
                      irecv.at[r], at(x, yl, 1))

    def share1(r):
        return remote(out_ref.at[2 * OCC + r], out_ref.at[3 * OCC + r], fsend.at[r],
                      frecv.at[r], at(x, yl, 0))

    def finish_around(r):
        return remote(relay_ref.at[r], out_ref.at[3 * OCC + r], wsend.at[r], frecv.at[r],
                      at(x + 1, yl, 1))

    def finish_detour(r):
        return remote(relay_ref.at[r], out_ref.at[2 * OCC + r], wsend.at[r], brecv.at[r],
                      at(3, yl, 1))

    def compute(r):
        fetch(r).wait()
        if r + 1 < OCC:
            fetch(r + 1).start()
        xs = xbuf.at[r % 2]

        def columns(n, _):
            c0 = pl.multiple_of(n * 256, 256)
            for h in range(2):
                half = NQ // 2
                part = xs[half * h:half * (h + 1)].reshape(half * rows, xs.shape[2])
                y = jnp.dot(part, coef_ref[:, pl.ds(c0, 256)],
                            preferred_element_type=jnp.float32)
                ybuf[half * h:half * (h + 1), :, pl.ds(c0, 256)] = y.astype(
                    jnp.bfloat16).reshape(half, rows, 256)
            return _

        lax.fori_loop(0, nvall // 256, columns, 0)

        def select(g, _):
            dom = dom_ref[r * NQ + g]
            def tile(n, acc):
                c0 = pl.multiple_of(n * 256, 256)
                ids = lax.broadcasted_iota(jnp.int32, (256, nvir), 0) + n * 256
                hot = jnp.where(ids == dom, 1.0, 0.0).astype(jnp.bfloat16)
                return acc + jnp.dot(ybuf[g, :, pl.ds(c0, 256)], hot,
                                     preferred_element_type=jnp.float32)
            acc = lax.fori_loop(0, nvall // 256, tile,
                                jnp.zeros((rows, nvir), jnp.float32))
            for b in range(rows // BLK):
                m = mask_ref[b, g * OCC + r].astype(jnp.float32)
                cbuf[r, g, b * BLK:(b + 1) * BLK, :] = (
                    acc[b * BLK:(b + 1) * BLK] * m).astype(jnp.bfloat16)
            return _

        lax.fori_loop(0, NQ, select, 0)

    fetch(0).start()
    first = jnp.logical_and(core == 1, x == 0)
    other = jnp.logical_not(first)
    for s in range(OCC + 2):
        if s < OCC:
            compute(s)
            keep(s).start()
            for d in range(1, NQ):
                exchange(s, d).start()
        if 1 <= s <= OCC:
            r = s - 1
            keep(r).wait()
            for d in range(1, NQ):
                exchange(r, d).wait_recv()

            @pl.when(core == 0)
            def _():
                around(r).start()

            @pl.when(first)
            def _():
                detour(r).start()

            @pl.when(other)
            def _():
                onward(r).start()

            @pl.when(core == 1)
            def _():
                to_core0(r).start()
        if s >= 2:
            r = s - 2

            @pl.when(core == 0)
            def _():
                around(r).wait_recv()
                finish_around(r).start()

            @pl.when(first)
            def _():
                detour(r).wait_recv()
                finish_detour(r).start()

            onward(r).wait_recv()

            @pl.when(core == 0)
            def _():
                share0(r).start()

            @pl.when(core == 1)
            def _():
                share1(r).start()

    for r in range(OCC):
        to_core0(r).wait_recv()
        share1(r).wait_recv()
        for d in range(1, NQ):
            exchange(r, d).wait_send()

        @pl.when(core == 0)
        def _():
            around(r).wait_send()
            finish_around(r).wait_send()
            share0(r).wait_send()

        @pl.when(first)
        def _():
            detour(r).wait_send()
            finish_detour(r).wait_send()

        @pl.when(other)
        def _():
            onward(r).wait_send()

        @pl.when(core == 1)
        def _():
            to_core0(r).wait_send()
            share1(r).wait_send()


def gather_partners(x, mask, coef, dom):
    _, _, rows, nbas = x.shape
    nvir = dom.shape[2]
    nvall = coef.shape[1]
    whole = jax.ShapeDtypeStruct((K * OCC, NQ * rows, nvir), jnp.bfloat16)
    relay = jax.ShapeDtypeStruct((OCC, NQ * rows, nvir), jnp.bfloat16)
    dma = pltpu.SemaphoreType.DMA
    return pl.pallas_call(
        gather_kernel,
        out_shape=(whole, relay),
        in_specs=[
            pl.BlockSpec(memory_space=pltpu.SMEM),
            pl.BlockSpec(memory_space=pl.ANY),
            pl.BlockSpec(memory_space=pltpu.VMEM),
            pl.BlockSpec(memory_space=pltpu.VMEM),
        ],
        out_specs=(pl.BlockSpec(memory_space=pl.ANY), pl.BlockSpec(memory_space=pl.ANY)),
        scratch_shapes=[
            pltpu.VMEM((2, NQ, rows, nbas), jnp.bfloat16),
            pltpu.VMEM((NQ, rows, nvall), jnp.bfloat16),
            pltpu.VMEM((OCC, NQ, rows, nvir), jnp.bfloat16),
            dma((2,)), dma((OCC,)),
            dma((OCC, NQ - 1)), dma((OCC, NQ - 1)),
            dma((OCC,)), dma((OCC,)),
            dma((OCC,)), dma((OCC,)),
            dma((OCC,)), dma((OCC,)),
            dma((OCC,)), dma((OCC,)),
            dma((OCC,)), dma((OCC,)),
        ],
        compiler_params=pltpu.CompilerParams(has_side_effects=True, vmem_limit_bytes=40 << 20),
        name="transform_exchange",
    )(mask, x, coef, dom)[0]


def pair_kernel(count_ref, code_ref, occ_ref, ints_ref, dom_ref, vir_ref, out_ref,
                own, partner, total, energy, order, osem, psem, dsem):
    n_aux = ints_ref.shape[1]
    nvir = ints_ref.shape[2]
    count = count_ref[0, 0]
    span = K * OCC

    def load_own(t):
        return pltpu.make_async_copy(ints_ref.at[t], own.at[0], osem.at[0])

    def load_partner(n):
        ku = code_ref[0, 0, order[n]] % span
        return pltpu.make_async_copy(ints_ref.at[ku], partner.at[n % 2], psem.at[n % 2])

    low = dom_ref[...] % 128
    high = dom_ref[...] // 128
    for row in range(0, span, 8):
        for c in range(0, nvir, 128):
            lo = low[row:row + 8, c:c + 128]
            hi = high[row:row + 8, c:c + 128]
            acc = jnp.zeros((8, 128), jnp.float32)
            for b in range(vir_ref.shape[0]):
                table = jnp.broadcast_to(vir_ref[b:b + 1, :], (8, 128))
                picked = jnp.take_along_axis(table, lo, axis=1)
                acc = jnp.where(hi == b, picked, acc)
            energy[row:row + 8, c:c + 128] = acc

    def per_own(t, start):
        def scan(s, n):
            hit = jnp.logical_and(s < count, code_ref[0, 0, s] // span == t)

            @pl.when(hit)
            def _():
                order[n] = s
            return n + hit.astype(jnp.int32)

        n_pairs = lax.fori_loop(0, code_ref.shape[2], scan, 0)
        load_own(t).start()

        @pl.when(n_pairs > 0)
        def _():
            load_partner(0).start()

        total[...] = jnp.zeros_like(total)
        load_own(t).wait()
        own[1] = own[0]
        occ_i = occ_ref[t]
        column = jnp.transpose(jnp.broadcast_to(energy[pl.ds(t, 1), :], (128, nvir)))

        def pair(n, carry):
            load_partner(n).wait()

            @pl.when(n + 1 < n_pairs)
            def _():
                load_partner(n + 1).start()

            ku = code_ref[0, 0, order[n]] % span
            held = partner.at[n % 2]
            ex = lax.dot_general(own[0], held[...], (((0,), (0,)), ((), ())),
                                 preferred_element_type=jnp.float32)
            denom = (jnp.concatenate([column] * (nvir // 128), axis=1)
                     + energy[pl.ds(ku, 1), :] - occ_i - occ_ref[ku])
            amp = (ex / denom).astype(jnp.bfloat16)
            total[...] += lax.dot_general(held[...], amp, (((1,), (1,)), ((), ())),
                                          preferred_element_type=jnp.float32)
            return carry

        lax.fori_loop(0, n_pairs, pair, 0)

        @pl.when(t > 0)
        def _():
            pltpu.make_async_copy(own.at[1], out_ref.at[0], dsem).wait()
        own[1] = total[...].astype(jnp.bfloat16)
        pltpu.make_async_copy(own.at[1], out_ref.at[t], dsem).start()
        return start

    lax.fori_loop(0, OCC, per_own, 0)
    pltpu.make_async_copy(own.at[1], out_ref.at[0], dsem).wait()


def pair_density(count, codes, occ, ints, dom, vir):
    span, n_aux, nvir = ints.shape
    smem = pl.BlockSpec(memory_space=pltpu.SMEM)
    vmem = pl.BlockSpec(memory_space=pltpu.VMEM)
    dma = pltpu.SemaphoreType.DMA
    return pl.pallas_call(
        pair_kernel,
        out_shape=jax.ShapeDtypeStruct((OCC, n_aux, nvir), jnp.bfloat16),
        in_specs=[smem, smem, smem, pl.BlockSpec(memory_space=pl.ANY), vmem, vmem],
        out_specs=pl.BlockSpec(memory_space=pl.ANY),
        scratch_shapes=[
            pltpu.VMEM((2, n_aux, nvir), jnp.bfloat16),
            pltpu.VMEM((2, n_aux, nvir), jnp.bfloat16),
            pltpu.VMEM((n_aux, nvir), jnp.float32),
            pltpu.VMEM((span, nvir), jnp.float32),
            pltpu.SMEM((codes.shape[2],), jnp.int32),
            dma((1,)), dma((2,)), dma(()),
        ],
        compiler_params=pltpu.CompilerParams(vmem_limit_bytes=40 << 20),
        name="pair_density",
    )(count, codes, occ, ints, dom, vir)


def body(half_ints, block_mask, vir_coef, domains, vir_energy, occ_energy, pair_count, pair_code):
    aux_count = lax.axis_size("aux")
    occ_count = lax.axis_size("occ")
    aux_pos = lax.axis_index("aux")
    occ_pos = lax.axis_index("occ")
    rows, local, nbas = half_ints.shape
    nvir = domains.shape[1]
    x = half_ints.reshape(rows, NQ, OCC, nbas).transpose(2, 1, 0, 3)
    own_domains = lax.dynamic_slice_in_dim(domains, occ_pos * local, local, 0)
    dom = own_domains.reshape(NQ, OCC, nvir).transpose(1, 0, 2).reshape(local, 1, nvir)
    ints = gather_partners(x, block_mask, vir_coef, dom)
    dom_rows = []
    occ_rows = []
    for offset in range(K):
        start = ((occ_pos + offset) % occ_count * aux_count + aux_pos) * OCC
        dom_rows.append(lax.dynamic_slice_in_dim(domains, start, OCC, 0))
        occ_rows.append(lax.dynamic_slice_in_dim(occ_energy, start, OCC, 0))
    density = pair_density(
        pair_count, pair_code, jnp.concatenate(occ_rows), ints,
        jnp.concatenate(dom_rows, axis=0), vir_energy.reshape(-1, 128))
    split = density.reshape(OCC, NQ, rows, nvir)
    back = lax.all_to_all(split, "aux", split_axis=1, concat_axis=1, tiled=True)
    return back.transpose(2, 1, 0, 3).reshape(rows, local, nvir)


def solution(mesh):
    placed = (
        P("aux", "occ", None),
        P("aux", "occ"),
        P(),
        P(),
        P(),
        P(),
        P("occ", "aux"),
        P("occ", "aux", None),
    )
    return jax.shard_map(
        body, mesh=mesh, in_specs=placed, out_specs=P("aux", "occ", None), check_vma=False
    )
```

time: 596 us -> 283 us (0.47)
  the two profiles are of different devices: /device:TPU:1 before, /device:TPU:5 now
where the time goes in v1:
time: 283 us; the launch traced here: 280 us
  Pallas kernels  185 us (65%)
  blocking collectives  65.5 us (23%)
  local copies, waits for them, and re-layouts  28.4 us (10%)
    pallas_call x1, Pallas kernels, gather_partners(): pl.pallas_call(gather_kernel, out_shape=(whole, relay), in_specs=[pl.Bloc...  159 us
    all_to_all x1, blocking collectives, body(): back = lax.all_to_all(split, 'aux', split_axis=1, concat_axis=1, tiled=True)  65.5 us
    pallas_call x1, Pallas kernels, pair_density(): pl.pallas_call(pair_kernel, out_shape=jax.ShapeDtypeStruct((OCC, n_aux, n...  25.7 us
    unnamed x11, local copies, waits for them, and re-layouts  13.5 us
    reshape x1, local copies, waits for them, and re-layouts, body(): x = half_ints.reshape(rows, NQ, OCC, nbas).transpose(2, 1, 0, 3)  8.23 us

profile of v1, /device:TPU:5, one launch (start us, length us, event | category | flops | bytes accessed | tf_op | source)
XLA Modules:
  0.0 279.6 jit_solution(15785775314328700734)
XLA Ops:
  0.7 11.3 %copy.14 = bf16[128,32,1024]{2,0,1:T(8,128)(2,1)} copy(bf16[128,32,1024]{2,1,0:T(8,128)(2,1)} %param.8) | data formatting | bytes 16777216 | tf_op args[0]
  12.0 0.0 copy-start.4
  12.0 0.0 copy-start.2
  12.0 8.2 %copy.20 = bf16[128,8,4,1024]{3,0,1,2:T(8,128)(2,1)} copy(bf16[128,8,4,1024]{3,0,2,1:T(8,128)(2,1)} %bitcast.13) | data formatting | bytes 16777216 | tf_op jit(solution)/shard_map/reshape | solution.py:345
  20.2 0.0 copy-done.4
  20.2 0.1 fusion
  20.3 0.8 constant_dynamic-slice_fusion.3
  21.1 0.9 constant_dynamic-slice_fusion.4
  22.0 0.1 reshape.20.dom_ref
  22.1 0.1 pad_maximum_fusion.occ_ref
  22.1 0.0 copy-done.2
  22.2 0.0 copy-start
  22.2 2.2 copy-done
  24.3 0.0 copy-start.1
  24.3 0.0 copy-start.3
  24.3 159.2 %transform_exchange.1 = (bf16[16,1024,512]{2,1,0:T(8,128)(2,1)}, bf16[4,1024,512]{2,1,0:T(8,128)(2,1)}) custom-call(s32[2,32]{1,0:T(2,128)S(1)} %copy-done.2, bf16[4,8,128,1024]{3,2,1,0:T(8,128)(2,1)} %bitcast.12, bf16[1024,2048]{1,0:T(8,128)(2,1)S(1)} %copy-done, s32[32,1,512]{2,1,0:T(1,128)S(1)} %reshape.20.dom_ref), custom_call_target="tpu_custom_call" | custom-call | tf_op jit(solution)/shard_map/transform_exchange/pallas_call | solution.py:208
  183.6 0.0 copy-done.1
  183.6 0.0 copy-done.3
  183.6 25.7 %pair_density.1 = bf16[4,1024,512]{2,1,0:T(8,128)(2,1)S(1)} custom-call(s32[1,1]{1,0:T(1,128)S(6)} %copy.21.count_ref, s32[1,1,16]{2,1,0:T(1,128)S(1)} %copy-done.3, f32[16]{0:T(128)S(1)} %pad_maximum_fusion.occ_ref, bf16[16,1024,512]{2,1,0:T(8,128)(2,1)} %get-tuple-element.6.ints_ref, s32[16,512]{1,0:T(8,128)S(1)} %pad_add_fusion.dom_ref, ...), custom_call_target="tpu_custom_call" | custom-call | tf_op jit(solution)/shard_map/pair_density/pallas_call | solution.py:320
  209.3 0.4 copy.17
  209.7 65.5 %all_to_all.5 = bf16[4,8,128,512]{3,2,0,1:T(8,128)(2,1)S(1)} all-to-all(bf16[4,8,128,512]{3,2,0,1:T(8,128)(2,1)S(1)} %copy.17), channel_id=1, replica_groups=mesh['aux'=8,'occ'=16] {'aux'}, dimensions={1} | all-to-all | bytes 8388608 | tf_op jit(solution)/shard_map/all_to_all | solution.py:359
  275.2 4.4 %copy.18 = bf16[128,32,512]{2,1,0:T(8,128)(2,1)} copy(bf16[128,32,512]{2,0,1:T(8,128)(2,1)S(1)} %bitcast.14) | data formatting | bytes 8388608 | tf_op jit(solution)/shard_map/reshape | solution.py:360
  (3 shorter events, 0.1 us)
Async XLA Ops:
  12.0 8.2 %copy-start.4 = (f32[512]{0:T(512)S(1)}, f32[512]{0:T(512)}, u32[]{:S(2)}) copy-start(f32[512]{0:T(512)} %param.13) | copy-start | bytes 6148
  12.0 10.2 %copy-start.2 = (s32[2,32]{1,0:T(2,128)S(1)}, s32[2,32]{1,0:T(2,128)}, u32[]{:S(2)}) copy-start(s32[2,32]{1,0:T(2,128)} %mask_ref.1) | copy-start | bytes 772
  22.2 2.2 copy-start
  24.3 159.2 %copy-start.1 = (f32[2048]{0:T(1024)S(1)}, f32[2048]{0:T(1024)}, u32[]{:S(2)}) copy-start(f32[2048]{0:T(1024)} %param.12) | copy-start | bytes 24580
  24.3 159.2 %copy-start.3 = (s32[1,1,16]{2,1,0:T(1,128)S(1)}, s32[1,1,16]{2,1,0:T(1,128)}, u32[]{:S(2)}) copy-start(s32[1,1,16]{2,1,0:T(1,128)} %code_ref.1) | copy-start | bytes 196

commit v2 on v0

v2 whole, which is shorter than its diff:
```python
import functools

import jax
import jax.numpy as jnp
from jax import lax
from jax.experimental import pallas as pl
from jax.experimental.pallas import tpu as pltpu
from jax.sharding import PartitionSpec as P

BLK = 64
OCC = 4
K = 4
NQ = 8
MESH = pl.DeviceIdType.MESH


def peer(q, d):
    return (q // 4 + d % 2) % 2 * 4 + (q + d // 2) % 4


def meet(devices):
    barrier = pltpu.get_barrier_semaphore()
    for device in devices:
        pl.semaphore_signal(barrier, inc=1, device_id=device, device_id_type=MESH)
    pl.semaphore_wait(barrier, len(devices))


def gather_kernel(mask_ref, x_ref, coef_ref, dom_ref, out_ref, relay_ref,
                  raw, xall, ybuf, cbuf, ids, doms, dsem, xsem, lsem, asend, arecv, bsend, brecv,
                  rsend, rrecv, isend, irecv, fsend, frecv, wsend):
    q = lax.axis_index("aux")
    o = lax.axis_index("occ")
    core = o % 2
    x = (o // 2) % 4
    yl = o // 8
    rows = x_ref.shape[0]
    nbas = x_ref.shape[2]
    nvall = coef_ref.shape[1]
    nvir = out_ref.shape[-1]
    tile = 256
    prev_y = jnp.where(x == 0, 1 - yl, yl)
    relay_y = jnp.where(x >= 2, yl, 1 - yl)
    first = jnp.logical_and(core == 1, x == 0)
    other = jnp.logical_not(first)

    def at(xx, yy, cc):
        return (q, (yy * 4 + xx % 4) * 2 + cc)

    def remote(src, dst, ssem, rsem, dev):
        return pltpu.make_async_remote_copy(
            src_ref=src, dst_ref=dst, send_sem=ssem, recv_sem=rsem,
            device_id=dev, device_id_type=MESH)

    def fetch(g):
        return pltpu.make_async_copy(x_ref.at[pl.ds(g * 16, 16)], raw.at[g], xsem.at[g])

    def exchange(r, h, d):
        to = peer(q, d)
        return remote(cbuf.at[r, h, to], out_ref.at[r, h, q],
                      asend.at[r, h, d - 1], arecv.at[r, h, d - 1], (to, o))

    def keep(r, h):
        return pltpu.make_async_copy(cbuf.at[r, h, q], out_ref.at[r, h, q], lsem.at[r, h])

    def onward(r, h):
        return remote(out_ref.at[r, h], out_ref.at[2 * OCC + r, h], bsend.at[r, h],
                      brecv.at[r, h], at(x + 3, prev_y, core))

    def detour(r, h):
        return remote(out_ref.at[r, h], relay_ref.at[r, h], rsend.at[r, h], rrecv.at[r, h],
                      at(0, 1 - yl, 1))

    def around(r, h):
        return remote(out_ref.at[r, h], relay_ref.at[r, h], rsend.at[r, h], rrecv.at[r, h],
                      at(x + 1, relay_y, 0))

    def to_core0(r, h):
        return remote(out_ref.at[r, h], out_ref.at[OCC + r, h], isend.at[r, h],
                      irecv.at[r, h], at(x, yl, 0))

    def share0(r, h):
        return remote(out_ref.at[2 * OCC + r, h], out_ref.at[OCC + r, h], fsend.at[r, h],
                      irecv.at[r, h], at(x, yl, 1))

    def share1(r, h):
        return remote(out_ref.at[2 * OCC + r, h], out_ref.at[3 * OCC + r, h],
                      fsend.at[r, h], frecv.at[r, h], at(x, yl, 0))

    def finish_around(r, h):
        return remote(relay_ref.at[r, h], out_ref.at[3 * OCC + r, h], wsend.at[r, h],
                      frecv.at[r, h], at(x + 1, yl, 1))

    def finish_detour(r, h):
        return remote(relay_ref.at[r, h], out_ref.at[2 * OCC + r, h], wsend.at[r, h],
                      brecv.at[r, h], at(3, yl, 1))

    def regroup():
        size = 8 * NQ * OCC
        row = lax.broadcasted_iota(jnp.int32, (size, size), 0)
        col = lax.broadcasted_iota(jnp.int32, (size, size), 1)
        source = (row % 8) * (NQ * OCC) + ((row // 8) % NQ) * OCC + row // (8 * NQ)
        moved = jnp.where(col == source, 1.0, 0.0).astype(jnp.bfloat16)
        ids[...] = lax.broadcasted_iota(jnp.int32, ids.shape, 0).astype(
            jnp.float32).astype(jnp.bfloat16)

        def group(g, carry):
            fetch(g).wait()
            halves = []
            for half in range(2):
                part = raw[g, 8 * half:8 * half + 8].reshape(size, nbas)
                halves.append(jnp.dot(moved, part, preferred_element_type=jnp.float32)
                              .reshape(NQ * OCC, 8, nbas))
            xall[:, pl.ds(pl.multiple_of(g * 16, 16), 16), :] = jnp.concatenate(
                halves, axis=1).astype(jnp.bfloat16)
            return carry

        lax.fori_loop(0, rows // 16, group, 0)

    def transform(r):
        def columns(n, carry):
            c0 = pl.multiple_of(n * tile, tile)
            for h in range(2):
                half = NQ // 2
                g0 = r * NQ + half * h
                part = xall[g0:g0 + half].reshape(half * rows, nbas)
                y = jnp.dot(part, coef_ref[:, pl.ds(c0, tile)],
                            preferred_element_type=jnp.float32)
                ybuf[half * h:half * (h + 1), :, pl.ds(c0, tile)] = y.astype(
                    jnp.bfloat16).reshape(half, rows, tile)
            return carry

        lax.fori_loop(0, nvall // tile, columns, 0)

    def select(r):
        def orbital(g, carry):
            dom = doms[pl.ds(g * OCC + r, 1), :]
            hot = []
            for n in range(nvall // tile):
                near = dom - n * tile
                inside = jnp.logical_and(near >= 0, near < tile)
                near = jnp.where(inside, near, -1).astype(jnp.float32).astype(jnp.bfloat16)
                hot.append(jnp.where(ids[...] == near, jnp.bfloat16(1), jnp.bfloat16(0)))
            acc = jnp.dot(ybuf[g], jnp.concatenate(hot, axis=0),
                          preferred_element_type=jnp.float32)
            for b in range(rows // BLK):
                m = mask_ref[b, g * OCC + r].astype(jnp.float32)
                cbuf[r, b, g] = (acc[b * BLK:(b + 1) * BLK] * m).astype(jnp.bfloat16)
            return carry

        lax.fori_loop(0, NQ, orbital, 0)
        for h in range(2):
            for d in range(1, NQ):
                exchange(r, h, d).start()
            keep(r, h).start()

    def send_on(r, h):
        keep(r, h).wait()
        for d in range(1, NQ):
            exchange(r, h, d).wait_recv()

        @pl.when(core == 0)
        def _():
            around(r, h).start()

        @pl.when(first)
        def _():
            detour(r, h).start()

        @pl.when(other)
        def _():
            onward(r, h).start()

        @pl.when(core == 1)
        def _():
            to_core0(r, h).start()

    def forward(r, h):
        @pl.when(core == 0)
        def _():
            around(r, h).wait_recv()
            finish_around(r, h).start()

        @pl.when(first)
        def _():
            detour(r, h).wait_recv()
            finish_detour(r, h).start()

        onward(r, h).wait_recv()

        @pl.when(core == 0)
        def _():
            share0(r, h).start()

        @pl.when(core == 1)
        def _():
            share1(r, h).start()

    mine = pltpu.make_async_copy(
        dom_ref.at[pl.ds(pl.multiple_of(o * doms.shape[0], 8), doms.shape[0])], doms, dsem)
    mine.start()
    for g in range(rows // 16):
        fetch(g).start()
    regroup()
    mine.wait()
    n_occ = lax.axis_size("occ")
    meet([(peer(q, d), o) for d in range(1, NQ)]
         + [(q, (o + d) % n_occ) for d in range(1, n_occ)])
    for s in range(OCC + 2):
        for h in range(2):
            if s < OCC and h == 0:
                transform(s)
            if s < OCC and h == 1:
                select(s)
            if 1 <= s <= OCC:
                send_on(s - 1, h)
            if s >= 2:
                forward(s - 2, h)

    for r in range(OCC):
        for h in range(2):
            to_core0(r, h).wait_recv()
            share1(r, h).wait_recv()
            for d in range(1, NQ):
                exchange(r, h, d).wait_send()

            @pl.when(core == 0)
            def _():
                around(r, h).wait_send()
                finish_around(r, h).wait_send()
                share0(r, h).wait_send()

            @pl.when(first)
            def _():
                detour(r, h).wait_send()
                finish_detour(r, h).wait_send()

            @pl.when(other)
            def _():
                onward(r, h).wait_send()

            @pl.when(core == 1)
            def _():
                to_core0(r, h).wait_send()
                share1(r, h).wait_send()


def gather_partners(x, mask, coef, dom):
    rows, local, nbas = x.shape
    nvir = dom.shape[1]
    nvall = coef.shape[1]
    halves = rows // BLK
    whole = jax.ShapeDtypeStruct((K * OCC, halves, NQ, BLK, nvir), jnp.bfloat16)
    relay = jax.ShapeDtypeStruct((OCC, halves, NQ, BLK, nvir), jnp.bfloat16)
    dma = pltpu.SemaphoreType.DMA
    return pl.pallas_call(
        gather_kernel,
        out_shape=(whole, relay),
        in_specs=[
            pl.BlockSpec(memory_space=pltpu.SMEM),
            pl.BlockSpec(memory_space=pl.ANY),
            pl.BlockSpec(memory_space=pltpu.VMEM),
            pl.BlockSpec(memory_space=pl.ANY),
        ],
        out_specs=(pl.BlockSpec(memory_space=pl.ANY), pl.BlockSpec(memory_space=pl.ANY)),
        scratch_shapes=[
            pltpu.VMEM((rows // 16, 16, local, nbas), jnp.bfloat16),
            pltpu.VMEM((local, rows, nbas), jnp.bfloat16),
            pltpu.VMEM((NQ, rows, nvall), jnp.bfloat16),
            pltpu.VMEM((OCC, halves, NQ, BLK, nvir), jnp.bfloat16),
            pltpu.VMEM((256, nvir), jnp.bfloat16),
            pltpu.VMEM((local, nvir), jnp.int32), dma(()),
            dma((rows // 16,)), dma((OCC, halves)),
            dma((OCC, halves, NQ - 1)), dma((OCC, halves, NQ - 1)),
        ] + [dma((OCC, halves))] * 9,
        compiler_params=pltpu.CompilerParams(collective_id=0, has_side_effects=True,
                                             vmem_limit_bytes=48 << 20),
        name="transform_exchange",
    )(mask, x, coef, dom)[0]


def pair_kernel(slot_ref, occ_ref, ints_ref, dom_ref, vir_ref, out_ref,
                parts, own, column, energy, doms, amp, run, snap, outbox, dsem, psem, lsem, ssem, rsem):
    q = lax.axis_index("aux")
    o = lax.axis_index("occ")
    span, n_aux, nvir = parts.shape
    pieces = outbox.shape[0]
    wide = nvir // pieces
    slots = slot_ref.shape[1]

    n_occ = lax.axis_size("occ")
    low_half = (q % 2) * OCC

    def landing(c):
        return out_ref.at[q, :, :, :, pl.ds(c * wide, wide)]

    def row_of(ku):
        return (ku // OCC) * 8 + low_half + ku % OCC

    def occupied(ku):
        return occ_ref[((o + ku // OCC) % n_occ * NQ + q) * OCC + ku % OCC]

    def names(k):
        first = ((o + k) % n_occ * NQ + q) // 2 * 8
        return pltpu.make_async_copy(dom_ref.at[pl.ds(pl.multiple_of(first, 8), 8)],
                                     doms.at[k], dsem.at[k])

    def load(j):
        return pltpu.make_async_copy(ints_ref.at[j], parts.at[j], psem.at[j])

    def send(c, d):
        to = peer(q, d)
        return pltpu.make_async_remote_copy(
            src_ref=outbox.at[c, to], dst_ref=landing(c), send_sem=ssem.at[c, d - 1],
            recv_sem=rsem.at[c, d - 1], device_id=(to, o), device_id_type=MESH)

    def keep(c):
        return pltpu.make_async_copy(outbox.at[c, q], landing(c), lsem.at[c])

    for k in range(K):
        names(k).start()
    for j in range(span):
        load(j).start()
    meet([(peer(q, d), o) for d in range(1, NQ)])
    for k in range(K):
        names(k).wait()
        low = doms[k] % 128
        high = doms[k] // 128
        for c in range(0, nvir, 128):
            acc = jnp.zeros((8, 128), jnp.float32)
            for b in range(vir_ref.shape[0]):
                table = jnp.broadcast_to(vir_ref[b:b + 1, :], (8, 128))
                picked = jnp.take_along_axis(table, low[:, c:c + 128], axis=1)
                acc = jnp.where(high[:, c:c + 128] == b, picked, acc)
            for i in range(8):
                energy[k * 8 + i, :, c:c + 128] = acc[i:i + 1]
    for t in range(OCC):
        column[t] = jnp.transpose(jnp.broadcast_to(energy[row_of(t)], (128, nvir)))
    for t in range(OCC):
        load(t).wait()

    def flip(t, carry):
        for c in range(pieces):
            own[t, c] = jnp.transpose(parts[t, :, c * wide:(c + 1) * wide])
        return carry

    lax.fori_loop(0, OCC, flip, 0)
    for j in range(OCC, span):
        load(j).wait()

    for c in range(pieces):
        def amplitude(n):
            t = slot_ref[0, n]
            ku = slot_ref[1, n]
            ex = jnp.dot(own[t, c], parts[ku], preferred_element_type=jnp.float32)
            mine = column[t, c * wide:(c + 1) * wide, :]
            denom = (jnp.concatenate([mine] * (nvir // 128), axis=1) + energy[row_of(ku)]
                     - occupied(t) - occupied(ku))
            live = slot_ref[2, n].astype(jnp.float32)
            amp[n % 2] = (ex / denom * live).astype(jnp.bfloat16)

        def contract(n):
            add = lax.dot_general(parts[slot_ref[1, n]], amp[n % 2], (((1,), (1,)), ((), ())),
                                  preferred_element_type=jnp.float32)
            same = slot_ref[3, n].astype(jnp.float32)
            total = run[...] * same + add
            run[...] = total
            snap[n] = total.astype(jnp.bfloat16)

        run[...] = jnp.zeros_like(run)
        amplitude(0)

        def step(n, carry):
            contract(n - 1)
            amplitude(n)
            return carry

        lax.fori_loop(1, slots, step, 0)
        contract(slots - 1)
        for t in range(OCC):
            some = slot_ref[5, t].astype(jnp.float32).astype(jnp.bfloat16)
            last = snap[slot_ref[4, t]] * some
            for h in range(n_aux // (NQ * BLK)):
                for p in range(NQ):
                    r0 = (h * NQ + p) * BLK
                    outbox[c, p, t, h] = last[r0:r0 + BLK]
        for d in range(1, NQ):
            send(c, d).start()
        keep(c).start()
    for c in range(pieces):
        keep(c).wait()
        for d in range(1, NQ):
            send(c, d).wait()


def pair_density(slots, occ, ints, dom, vir, pieces):
    span, n_aux, nvir = ints.shape
    wide = nvir // pieces
    halves = n_aux // (NQ * BLK)
    smem = pl.BlockSpec(memory_space=pltpu.SMEM)
    vmem = pl.BlockSpec(memory_space=pltpu.VMEM)
    dma = pltpu.SemaphoreType.DMA
    box = (pieces, NQ, OCC, halves, BLK, wide)
    return pl.pallas_call(
        pair_kernel,
        out_shape=jax.ShapeDtypeStruct((NQ, OCC, halves, BLK, nvir), jnp.bfloat16),
        in_specs=[smem, smem, pl.BlockSpec(memory_space=pl.ANY),
                  pl.BlockSpec(memory_space=pl.ANY), vmem],
        out_specs=pl.BlockSpec(memory_space=pl.ANY),
        scratch_shapes=[
            pltpu.VMEM((span, n_aux, nvir), jnp.bfloat16),
            pltpu.VMEM((OCC, pieces, wide, n_aux), jnp.bfloat16),
            pltpu.VMEM((OCC, nvir, 128), jnp.float32),
            pltpu.VMEM((2 * span, 1, nvir), jnp.float32),
            pltpu.VMEM((K, 8, nvir), jnp.int32),
            pltpu.VMEM((2, wide, nvir), jnp.bfloat16),
            pltpu.VMEM((n_aux, wide), jnp.float32),
            pltpu.VMEM((slots.shape[1], n_aux, wide), jnp.bfloat16),
            pltpu.VMEM(box, jnp.bfloat16),
            dma((K,)), dma((span,)), dma((pieces,)), dma((pieces, NQ - 1)), dma((pieces, NQ - 1)),
        ],
        compiler_params=pltpu.CompilerParams(collective_id=1, has_side_effects=True,
                                             vmem_limit_bytes=48 << 20),
        name="pair_density",
    )(slots, occ, ints, dom, vir)


def slot_kernel(count_ref, code_ref, out_ref):
    span = K * OCC
    cap = code_ref.shape[2]
    count = count_ref[0, 0]

    def clear(n, carry):
        out_ref[0, n] = 0
        out_ref[1, n] = 0
        out_ref[2, n] = 0
        out_ref[3, n] = 0
        return carry

    lax.fori_loop(0, cap, clear, 0)
    at = jnp.int32(0)
    for t in range(OCC):
        begin = at

        def scan(s, n):
            code = code_ref[0, 0, s]
            hit = code // span == t

            @pl.when(hit)
            def _():
                out_ref[0, n] = t
                out_ref[1, n] = code % span
                out_ref[2, n] = 1
                out_ref[3, n] = (n > begin).astype(jnp.int32)
            return n + hit.astype(jnp.int32)

        at = lax.fori_loop(0, count, scan, at)
        out_ref[4, t] = jnp.maximum(at - 1, 0)
        out_ref[5, t] = (at > begin).astype(jnp.int32)


def slot_table(count, codes):
    smem = pl.BlockSpec(memory_space=pltpu.SMEM)
    return pl.pallas_call(
        slot_kernel,
        out_shape=jax.ShapeDtypeStruct((6, codes.shape[2]), jnp.int32),
        in_specs=[smem, smem],
        out_specs=smem,
        name="slot_table",
    )(count, codes)


def body(half_ints, block_mask, vir_coef, domains, vir_energy, occ_energy, pair_count, pair_code):
    rows, local, _ = half_ints.shape
    nvir = domains.shape[1]
    ints = gather_partners(half_ints, block_mask, vir_coef, domains)
    density = pair_density(
        slot_table(pair_count, pair_code), occ_energy,
        ints.reshape(K * OCC, NQ * rows, nvir), domains, vir_energy.reshape(-1, 128), 2)
    return density.transpose(2, 3, 0, 1, 4).reshape(rows, local, nvir)


def solution(mesh):
    placed = (
        P("aux", "occ", None),
        P("aux", "occ"),
        P(),
        P(),
        P(),
        P(),
        P("occ", "aux"),
        P("occ", "aux", None),
    )
    return jax.shard_map(
        body, mesh=mesh, in_specs=placed, out_specs=P("aux", "occ", None), check_vma=False
    )
```

time: 596 us -> 223 us (0.37); the launches traced: 585 us -> 223 us
  Pallas kernels: 0 us -> 216 us
  local copies, waits for them, and re-layouts: 182 us -> 6.95 us
  matrix products: 121 us -> 0 us
  waiting for transfers between devices: 113 us -> 0 us
  blocking collectives: 84.6 us -> 0 us
  loops' own time: 47.6 us -> 0 us
  other arithmetic: 29 us -> 0 us
  starting transfers between devices: 7.91 us -> 0 us
    pallas_call x0 -> x3, Pallas kernels: none -> 216 us  [the longest x1 148 us: gather_partners(): pl.pallas_call(gather_kernel, out_shape=(whole, relay), in_specs=[pl.Bloc...]
    gather x3 -> x0, local copies, waits for them, and re-layouts: 129 us -> none  [the longest x1 83 us: body(): gathered_coef = jnp.take(vir_coef, own_domains, axis=1)]
    dot_general x17 -> x0, matrix products: 121 us -> none  [the longest x16 105 us: padded_step(): lax.dot_general(partner_rows, amplitude, (((1,), (1,)), ((), ())), prefer...]
    ppermute x3 -> x0, waiting for transfers between devices: 95.5 us -> none  [passed_along(): return lax.ppermute(value, axis, pairs)]
    all_to_all x2 -> x0, blocking collectives: 84.6 us -> none  [the longest x1 57.7 us: body(): lax.all_to_all(transformed, 'aux', split_axis=1, concat_axis=0, tiled=True)]
    another operation x1 -> x0, loops' own time: 47.6 us -> none  [body(): gamma = lax.fori_loop(0, codes.shape[0], padded_step, gamma)]
    dynamic_slice x50 -> x0, local copies, waits for them, and re-layouts: 20.1 us -> none  [the longest x16 9.88 us: padded_step(): partner_occ[own_slot]]
    all_to_all x1 -> x0, waiting for transfers between devices: 17.3 us -> none  [cut_exchange(): lax.all_to_all(piece, axis, split_axis=0, concat_axis=0, tiled=True)]
  transfers between devices with their start and end apart: 4 -> 0, of which waited for: 3 -> 0; matrix products, arithmetic and copies ran while one was open for 9% -> 0% of each run, Pallas kernels for 0% -> 0%
where the time goes in v2:
time: 223 us
  Pallas kernels  216 us (97%)
  local copies, waits for them, and re-layouts  6.95 us (3%)
    pallas_call x1, Pallas kernels, gather_partners(): pl.pallas_call(gather_kernel, out_shape=(whole, relay), in_specs=[pl.Bloc...  148 us
    pallas_call x1, Pallas kernels, pair_density(): pl.pallas_call(pair_kernel, out_shape=jax.ShapeDtypeStruct((NQ, OCC, halv...  64.8 us

profile of v2, /device:TPU:1, one launch (start us, length us, event | category | flops | bytes accessed | tf_op | source)
XLA Modules:
  0.0 223.2 jit_solution(803259524297066679)
XLA Ops:
  0.0 0.0 copy-start
  0.0 1.2 copy-done
  1.2 0.0 copy-start.5
  1.2 0.7 copy-done.5
  1.9 0.0 copy-start.1
  1.9 0.0 copy-start.3
  1.9 0.0 copy-start.4
  1.9 148.3 %transform_exchange.1 = (bf16[16,2,8,64,512]{4,3,2,1,0:T(8,128)(2,1)}, bf16[4,2,8,64,512]{4,3,2,1,0:T(8,128)(2,1)}) custom-call(s32[2,32]{1,0:T(2,128)S(1)} %copy-done.5, bf16[128,32,1024]{2,1,0:T(8,128)(2,1)} %x_ref.1, bf16[1024,2048]{1,0:T(8,128)(2,1)} %coef_ref.1, s32[512,512]{1,0:T(8,128)S(1)} %copy-done), custom_call_target="tpu_custom_call" | custom-call | tf_op jit(solution)/shard_map/transform_exchange/pallas_call | solution.py:255
  150.9 2.4 %slot_table.1.slot_ref = s32[6,16]{1,0:T(8,128)} custom-call(s32[1,1]{1,0:T(1,128)S(6)} %copy.10.count_ref, s32[1,1,16]{2,1,0:T(1,128)} %code_ref.1), custom_call_target="tpu_custom_call" | custom-call | tf_op jit(solution)/shard_map/slot_table/pallas_call | solution.py:463
  153.3 0.0 copy-done.1
  153.3 0.0 copy-done.3
  153.3 0.0 copy-done.4
  153.3 0.0 copy-start.2
  153.4 0.7 copy-done.2
  154.0 64.8 %pair_density.1 = bf16[8,4,2,64,512]{4,3,2,1,0:T(8,128)(2,1)S(1)} custom-call(s32[6,16]{1,0:T(8,128)S(1)} %copy-done.2, f32[512]{0:T(512)S(1)} %copy-done.4, bf16[16,1024,512]{2,1,0:T(8,128)(2,1)} %bitcast.7, s32[512,512]{1,0:T(8,128)S(1)} %copy-done.1, f32[16,128]{1,0:T(8,128)S(1)} %bitcast.6), custom_call_target="tpu_custom_call" | custom-call | tf_op jit(solution)/shard_map/pair_density/pallas_call | solution.py:403
  218.9 4.4 %copy.9 = bf16[128,32,512]{2,1,0:T(8,128)(2,1)} copy(bf16[128,32,512]{2,0,1:T(8,128)(2,1)S(1)} %bitcast.5) | data formatting | bytes 8388608 | tf_op jit(solution)/shard_map/reshape | solution.py:479
Async XLA Ops:
  0.0 1.2 copy-start
  1.2 0.7 copy-start.5
  1.9 151.4 %copy-start.1 = (s32[512,512]{1,0:T(8,128)S(1)}, s32[512,512]{1,0:T(8,128)}, u32[]{:S(2)}) copy-start(s32[512,512]{1,0:T(8,128)} %dom_ref.3) | copy-start | bytes 3145732
  1.9 151.4 %copy-start.3 = (f32[2048]{0:T(1024)S(1)}, f32[2048]{0:T(1024)}, u32[]{:S(2)}) copy-start(f32[2048]{0:T(1024)} %param.12) | copy-start | bytes 24580
  1.9 151.4 %copy-start.4 = (f32[512]{0:T(512)S(1)}, f32[512]{0:T(512)}, u32[]{:S(2)}) copy-start(f32[512]{0:T(512)} %occ_ref.1) | copy-start | bytes 6148
  153.3 0.7 copy-start.2

commit v3 on v2

v3 whole, which is shorter than its diff:
```python
import functools

import jax
import jax.numpy as jnp
from jax import lax
from jax.experimental import pallas as pl
from jax.experimental.pallas import tpu as pltpu
from jax.sharding import PartitionSpec as P

BLK = 64
OCC = 4
K = 4
NQ = 8
MESH = pl.DeviceIdType.MESH


def timeline():
    steps = []
    for s in range(OCC + 2):
        if s < OCC:
            steps.append(("transform", s, 0))
        if 1 <= s <= OCC:
            steps.append(("send", s - 1, 0))
        if s >= 2:
            steps += [("relay", s - 2, 1), ("share", s - 2, 0)]
        if s < OCC:
            steps.append(("select", s, 0))
        if 1 <= s <= OCC:
            steps += [("relay", s - 1, 0), ("send", s - 1, 1)]
        if s == OCC:
            steps.append(("prepare", 0, 0))
        if s >= 2:
            steps.append(("share", s - 2, 1))
    return steps


ORDER = timeline()


def peer(q, d):
    return (q // 4 + d % 2) % 2 * 4 + (q + d // 2) % 4


def meet(devices):
    barrier = pltpu.get_barrier_semaphore()
    for device in devices:
        pl.semaphore_signal(barrier, inc=1, device_id=device, device_id_type=MESH)
    pl.semaphore_wait(barrier, len(devices))


def fused_kernel(slot_ref, mask_ref, occ_ref, x_ref, coef_ref, dom_ref, vir_ref, out_ref,
                 relay_ref, parts, cbuf, outbox, own, column, energy, ids, doms, near,
                 dsem, xsem, lsem, asend, arecv, bsend, brecv, rsend, rrecv, isend, irecv,
                 fsend, frecv, wsend, nsem, ksem, ssem, dens_sem):
    q = lax.axis_index("aux")
    o = lax.axis_index("occ")
    core = o % 2
    x = (o // 2) % 4
    yl = o // 8
    rows = x_ref.shape[0]
    nbas = x_ref.shape[2]
    nvall = coef_ref.shape[1]
    nvir = parts.shape[-1]
    span = parts.shape[0]
    n_aux = rows * NQ
    n_occ = lax.axis_size("occ")
    low_half = (q % 2) * OCC
    tile = 256
    prev_y = jnp.where(x == 0, 1 - yl, yl)
    relay_y = jnp.where(x >= 2, yl, 1 - yl)
    first = jnp.logical_and(core == 1, x == 0)
    other = jnp.logical_not(first)

    def at(xx, yy, cc):
        return (q, (yy * 4 + xx % 4) * 2 + cc)

    def remote(src, dst, ssem, rsem, dev):
        return pltpu.make_async_remote_copy(
            src_ref=src, dst_ref=dst, send_sem=ssem, recv_sem=rsem,
            device_id=dev, device_id_type=MESH)

    def fetch(g, raw):
        return pltpu.make_async_copy(x_ref.at[pl.ds(g * 16, 16)], raw.at[g], xsem.at[g])

    def exchange(r, h, d):
        to = peer(q, d)
        return remote(cbuf.at[r, h, to], parts.at[r, h, q],
                      asend.at[r, h, d - 1], arecv.at[r, h, d - 1], (to, o))

    def keep(r, h):
        return pltpu.make_async_copy(cbuf.at[r, h, q], parts.at[r, h, q], lsem.at[r, h])

    def onward(r, h):
        return remote(parts.at[r, h], parts.at[2 * OCC + r, h], bsend.at[r, h],
                      brecv.at[r, h], at(x + 3, prev_y, core))

    def detour(r, h):
        return remote(parts.at[r, h], relay_ref.at[r, h], rsend.at[r, h], rrecv.at[r, h],
                      at(0, 1 - yl, 1))

    def around(r, h):
        return remote(parts.at[r, h], relay_ref.at[r, h], rsend.at[r, h], rrecv.at[r, h],
                      at(x + 1, relay_y, 0))

    def to_core0(r, h):
        return remote(parts.at[r, h], parts.at[OCC + r, h], isend.at[r, h],
                      irecv.at[r, h], at(x, yl, 0))

    def share0(r, h):
        return remote(parts.at[2 * OCC + r, h], parts.at[OCC + r, h], fsend.at[r, h],
                      irecv.at[r, h], at(x, yl, 1))

    def share1(r, h):
        return remote(parts.at[2 * OCC + r, h], parts.at[3 * OCC + r, h],
                      fsend.at[r, h], frecv.at[r, h], at(x, yl, 0))

    def finish_around(r, h):
        return remote(relay_ref.at[r, h], parts.at[3 * OCC + r, h], wsend.at[r, h],
                      frecv.at[r, h], at(x + 1, yl, 1))

    def finish_detour(r, h):
        return remote(relay_ref.at[r, h], parts.at[2 * OCC + r, h], wsend.at[r, h],
                      brecv.at[r, h], at(3, yl, 1))

    def regroup(raw, xall):
        size = 8 * NQ * OCC
        row = lax.broadcasted_iota(jnp.int32, (size, size), 0)
        col = lax.broadcasted_iota(jnp.int32, (size, size), 1)
        source = (row % 8) * (NQ * OCC) + ((row // 8) % NQ) * OCC + row // (8 * NQ)
        moved = jnp.where(col == source, 1.0, 0.0).astype(jnp.bfloat16)
        ids[...] = lax.broadcasted_iota(jnp.int32, ids.shape, 0).astype(
            jnp.float32).astype(jnp.bfloat16)

        def group(g, carry):
            fetch(g, raw).wait()
            halves = []
            for half in range(2):
                part = raw[g, 8 * half:8 * half + 8].reshape(size, nbas)
                halves.append(jnp.dot(moved, part, preferred_element_type=jnp.float32)
                              .reshape(NQ * OCC, 8, nbas))
            xall[:, pl.ds(pl.multiple_of(g * 16, 16), 16), :] = jnp.concatenate(
                halves, axis=1).astype(jnp.bfloat16)
            return carry

        lax.fori_loop(0, rows // 16, group, 0)

    def transform(r, xall, ybuf):
        def columns(n, carry):
            c0 = pl.multiple_of(n * tile, tile)
            for h in range(2):
                half = NQ // 2
                g0 = r * NQ + half * h
                part = xall[g0:g0 + half].reshape(half * rows, nbas)
                y = jnp.dot(part, coef_ref[:, pl.ds(c0, tile)],
                            preferred_element_type=jnp.float32)
                ybuf[half * h:half * (h + 1), :, pl.ds(c0, tile)] = y.astype(
                    jnp.bfloat16).reshape(half, rows, tile)
            return carry

        lax.fori_loop(0, nvall // tile, columns, 0)

    def select(r, ybuf):
        def orbital(g, carry):
            dom = doms[pl.ds(g * OCC + r, 1), :]
            hot = []
            for n in range(nvall // tile):
                near = dom - n * tile
                inside = jnp.logical_and(near >= 0, near < tile)
                near = jnp.where(inside, near, -1).astype(jnp.float32).astype(jnp.bfloat16)
                hot.append(jnp.where(ids[...] == near, jnp.bfloat16(1), jnp.bfloat16(0)))
            acc = jnp.dot(ybuf[g], jnp.concatenate(hot, axis=0),
                          preferred_element_type=jnp.float32)
            for b in range(rows // BLK):
                m = mask_ref[b, g * OCC + r].astype(jnp.float32)
                cbuf[r, b, g] = (acc[b * BLK:(b + 1) * BLK] * m).astype(jnp.bfloat16)
            return carry

        lax.fori_loop(0, NQ, orbital, 0)
        for h in range(2):
            for d in range(1, NQ):
                exchange(r, h, d).start()
            keep(r, h).start()

    def send_on(r, h):
        keep(r, h).wait()
        for d in range(1, NQ):
            exchange(r, h, d).wait_recv()

        @pl.when(core == 0)
        def _():
            around(r, h).start()

        @pl.when(first)
        def _():
            detour(r, h).start()

        @pl.when(other)
        def _():
            onward(r, h).start()

        @pl.when(core == 1)
        def _():
            to_core0(r, h).start()

    def relay(r, h):
        @pl.when(core == 0)
        def _():
            around(r, h).wait_recv()
            finish_around(r, h).start()

        @pl.when(first)
        def _():
            detour(r, h).wait_recv()
            finish_detour(r, h).start()

    def share(r, h):
        onward(r, h).wait_recv()

        @pl.when(core == 0)
        def _():
            share0(r, h).start()

        @pl.when(core == 1)
        def _():
            share1(r, h).start()

    pieces = outbox.shape[0]
    wide = nvir // pieces
    slots = slot_ref.shape[1]

    def landing(c):
        return out_ref.at[q, :, :, :, pl.ds(c * wide, wide)]

    def row_of(ku):
        return (ku // OCC) * 8 + low_half + ku % OCC

    def occupied(ku):
        return occ_ref[((o + ku // OCC) % n_occ * NQ + q) * OCC + ku % OCC]

    def names(k):
        first = ((o + k) % n_occ * NQ + q) // 2 * 8
        return pltpu.make_async_copy(dom_ref.at[pl.ds(pl.multiple_of(first, 8), 8)],
                                     near.at[k], nsem.at[k])

    def send(c, d):
        to = peer(q, d)
        return pltpu.make_async_remote_copy(
            src_ref=outbox.at[c, to], dst_ref=landing(c), send_sem=ssem.at[c, d - 1],
            recv_sem=dens_sem.at[c, d - 1], device_id=(to, o), device_id_type=MESH)

    def keep_box(c):
        return pltpu.make_async_copy(outbox.at[c, q], landing(c), ksem.at[c])

    def prepare():
        for k in range(K):
            names(k).wait()
            low = near[k] % 128
            high = near[k] // 128
            for c in range(0, nvir, 128):
                acc = jnp.zeros((8, 128), jnp.float32)
                for b in range(vir_ref.shape[0]):
                    table = jnp.broadcast_to(vir_ref[b:b + 1, :], (8, 128))
                    picked = jnp.take_along_axis(table, low[:, c:c + 128], axis=1)
                    acc = jnp.where(high[:, c:c + 128] == b, picked, acc)
                for i in range(8):
                    energy[k * 8 + i, :, c:c + 128] = acc[i:i + 1]
        for t in range(OCC):
            column[t] = jnp.transpose(jnp.broadcast_to(energy[row_of(t)], (128, nvir)))
        def flip(t, carry):
            for c in range(pieces):
                own[t, c] = jnp.transpose(
                    parts[t, :, :, :, c * wide:(c + 1) * wide].reshape(n_aux, wide))
            return carry

        lax.fori_loop(0, OCC, flip, 0)

    def densities(amp, run, snap):
        for c in range(pieces):
            def amplitude(n):
                t = slot_ref[0, n]
                ku = slot_ref[1, n]
                ex = jnp.dot(own[t, c], parts[ku].reshape(n_aux, nvir), preferred_element_type=jnp.float32)
                mine = column[t, c * wide:(c + 1) * wide, :]
                denom = (jnp.concatenate([mine] * (nvir // 128), axis=1) + energy[row_of(ku)]
                         - occupied(t) - occupied(ku))
                live = slot_ref[2, n].astype(jnp.float32)
                amp[n % 2] = (ex / denom * live).astype(jnp.bfloat16)

            def contract(n):
                add = lax.dot_general(parts[slot_ref[1, n]].reshape(n_aux, nvir), amp[n % 2], (((1,), (1,)), ((), ())),
                                      preferred_element_type=jnp.float32)
                same = slot_ref[3, n].astype(jnp.float32)
                total = run[...] * same + add
                run[...] = total
                snap[n] = total.astype(jnp.bfloat16)

            run[...] = jnp.zeros_like(run)
            amplitude(0)

            def step(n, carry):
                contract(n - 1)
                amplitude(n)
                return carry

            lax.fori_loop(1, slots, step, 0)
            contract(slots - 1)
            for t in range(OCC):
                some = slot_ref[5, t].astype(jnp.float32).astype(jnp.bfloat16)
                last = snap[slot_ref[4, t]] * some
                for h in range(n_aux // (NQ * BLK)):
                    for p in range(NQ):
                        r0 = (h * NQ + p) * BLK
                        outbox[c, p, t, h] = last[r0:r0 + BLK]
            for d in range(1, NQ):
                send(c, d).start()
            keep_box(c).start()

    mine = pltpu.make_async_copy(
        dom_ref.at[pl.ds(pl.multiple_of(o * doms.shape[0], 8), doms.shape[0])], doms, dsem)
    mine.start()
    for k in range(K):
        names(k).start()

    def collect(raw, xall, ybuf):
        for g in range(rows // 16):
            fetch(g, raw).start()
        regroup(raw, xall)
        mine.wait()
        meet([(peer(q, d), o) for d in range(1, NQ)]
             + [(q, (o + d) % n_occ) for d in range(1, n_occ)])
        for name, r, h in ORDER:
            if name == "transform":
                transform(r, xall, ybuf)
            if name == "select":
                select(r, ybuf)
            if name == "send":
                send_on(r, h)
            if name == "relay":
                relay(r, h)
            if name == "share":
                share(r, h)
            if name == "prepare":
                prepare()

    pl.run_scoped(
        collect,
        pltpu.VMEM((rows // 16, 16, doms.shape[0], nbas), jnp.bfloat16),
        pltpu.VMEM((doms.shape[0], rows, nbas), jnp.bfloat16),
        pltpu.VMEM((NQ, rows, nvall), jnp.bfloat16))
    for r in range(OCC):
        for h in range(2):
            to_core0(r, h).wait_recv()
            share1(r, h).wait_recv()
    pl.run_scoped(
        densities,
        pltpu.VMEM((2, wide, nvir), jnp.bfloat16),
        pltpu.VMEM((n_aux, wide), jnp.float32),
        pltpu.VMEM((slots, n_aux, wide), jnp.bfloat16))
    for c in range(pieces):
        keep_box(c).wait()
        for d in range(1, NQ):
            send(c, d).wait()
    for r in range(OCC):
        for h in range(2):
            for d in range(1, NQ):
                exchange(r, h, d).wait_send()

            @pl.when(core == 0)
            def _():
                around(r, h).wait_send()
                finish_around(r, h).wait_send()
                share0(r, h).wait_send()

            @pl.when(first)
            def _():
                detour(r, h).wait_send()
                finish_detour(r, h).wait_send()

            @pl.when(other)
            def _():
                onward(r, h).wait_send()

            @pl.when(core == 1)
            def _():
                to_core0(r, h).wait_send()
                share1(r, h).wait_send()


def fused(slots, mask, occ, x, coef, dom, vir, pieces):
    rows, local, nbas = x.shape
    nvir = dom.shape[1]
    halves = rows // BLK
    wide = nvir // pieces
    span = K * OCC
    smem = pl.BlockSpec(memory_space=pltpu.SMEM)
    vmem = pl.BlockSpec(memory_space=pltpu.VMEM)
    hbm = pl.BlockSpec(memory_space=pl.ANY)
    dma = pltpu.SemaphoreType.DMA
    unit = (halves, NQ, BLK, nvir)
    box = (pieces, NQ, OCC, halves, BLK, wide)
    return pl.pallas_call(
        fused_kernel,
        out_shape=(jax.ShapeDtypeStruct((NQ, OCC, halves, BLK, nvir), jnp.bfloat16),
                   jax.ShapeDtypeStruct((OCC,) + unit, jnp.bfloat16)),
        in_specs=[smem, smem, smem, hbm, vmem, hbm, vmem],
        out_specs=(hbm, hbm),
        scratch_shapes=[
            pltpu.VMEM((span,) + unit, jnp.bfloat16),
            pltpu.VMEM((OCC,) + unit, jnp.bfloat16),
            pltpu.VMEM(box, jnp.bfloat16),
            pltpu.VMEM((OCC, pieces, wide, NQ * rows), jnp.bfloat16),
            pltpu.VMEM((OCC, nvir, 128), jnp.float32),
            pltpu.VMEM((2 * span, 1, nvir), jnp.float32),
            pltpu.VMEM((256, nvir), jnp.bfloat16),
            pltpu.VMEM((local, nvir), jnp.int32),
            pltpu.VMEM((K, 8, nvir), jnp.int32),
            dma(()), dma((rows // 16,)), dma((OCC, halves)),
            dma((OCC, halves, NQ - 1)), dma((OCC, halves, NQ - 1)),
        ] + [dma((OCC, halves))] * 9 + [
            dma((K,)), dma((pieces,)), dma((pieces, NQ - 1)), dma((pieces, NQ - 1)),
        ],
        compiler_params=pltpu.CompilerParams(collective_id=0, has_side_effects=True,
                                             vmem_limit_bytes=63 << 20),
        name="pair_density",
    )(slots, mask, occ, x, coef, dom, vir)[0]


def slot_kernel(count_ref, code_ref, out_ref):
    span = K * OCC
    cap = code_ref.shape[2]
    count = count_ref[0, 0]

    def clear(n, carry):
        out_ref[0, n] = 0
        out_ref[1, n] = 0
        out_ref[2, n] = 0
        out_ref[3, n] = 0
        return carry

    lax.fori_loop(0, cap, clear, 0)
    at = jnp.int32(0)
    for t in range(OCC):
        begin = at

        def scan(s, n):
            code = code_ref[0, 0, s]
            hit = code // span == t

            @pl.when(hit)
            def _():
                out_ref[0, n] = t
                out_ref[1, n] = code % span
                out_ref[2, n] = 1
                out_ref[3, n] = (n > begin).astype(jnp.int32)
            return n + hit.astype(jnp.int32)

        at = lax.fori_loop(0, count, scan, at)
        out_ref[4, t] = jnp.maximum(at - 1, 0)
        out_ref[5, t] = (at > begin).astype(jnp.int32)


def slot_table(count, codes):
    smem = pl.BlockSpec(memory_space=pltpu.SMEM)
    return pl.pallas_call(
        slot_kernel,
        out_shape=jax.ShapeDtypeStruct((6, codes.shape[2]), jnp.int32),
        in_specs=[smem, smem],
        out_specs=smem,
        name="slot_table",
    )(count, codes)


def body(half_ints, block_mask, vir_coef, domains, vir_energy, occ_energy, pair_count, pair_code):
    rows, local, _ = half_ints.shape
    nvir = domains.shape[1]
    density = fused(slot_table(pair_count, pair_code), block_mask, occ_energy, half_ints,
                    vir_coef, domains, vir_energy.reshape(-1, 128), 2)
    return density.transpose(2, 3, 0, 1, 4).reshape(rows, local, nvir)


def solution(mesh):
    placed = (
        P("aux", "occ", None),
        P("aux", "occ"),
        P(),
        P(),
        P(),
        P(),
        P("occ", "aux"),
        P("occ", "aux", None),
    )
    return jax.shard_map(
        body, mesh=mesh, in_specs=placed, out_specs=P("aux", "occ", None), check_vma=False
    )
```

time: 223 us -> 205 us (0.919)
  the two profiles are of different devices: /device:TPU:1 before, /device:TPU:7 now
where the time goes in v3:
time: 205 us; the launch traced here: 204 us
  Pallas kernels  197 us (96%)
  local copies, waits for them, and re-layouts  6.54 us (3%)
    pallas_call x1, Pallas kernels, fused(): pl.pallas_call(fused_kernel, out_shape=(jax.ShapeDtypeStruct((NQ, OCC, ha...  195 us
    reshape x1, local copies, waits for them, and re-layouts, body(): return density.transpose(2, 3, 0, 1, 4).reshape(rows, local, nvir)  6.54 us

profile of v3, /device:TPU:7, one launch (start us, length us, event | category | flops | bytes accessed | tf_op | source)
XLA Modules:
  0.0 204.1 jit_solution(6370436054312817712)
XLA Ops:
  0.7 1.6 slot_table.1.slot_ref
  2.3 195.2 %pair_density.1 = (bf16[8,4,2,64,512]{4,3,2,1,0:T(8,128)(2,1)}, bf16[4,2,8,64,512]{4,3,2,1,0:T(8,128)(2,1)}) custom-call(s32[6,16]{1,0:T(8,128)} %slot_table.1.slot_ref, s32[2,32]{1,0:T(2,128)} %mask_ref.1, f32[512]{0:T(512)} %occ_ref.1, bf16[128,32,1024]{2,1,0:T(8,128)(2,1)} %x_ref.1, bf16[1024,2048]{1,0:T(8,128)(2,1)} %coef_ref.1, s32[512,512]{1,0:T(8,128)} %dom_ref.1, ...), custom_call_target="tpu_custom_call" | custom-call | tf_op jit(solution)/shard_map/pair_density/pallas_call | solution.py:401
  197.5 6.5 %copy.9 = bf16[128,32,512]{2,1,0:T(8,128)(2,1)} copy(bf16[128,32,512]{2,0,1:T(8,128)(2,1)} %bitcast.4) | data formatting | bytes 8388608 | tf_op jit(solution)/shard_map/reshape | solution.py:478

commit v4 on v3

--- a/solution.py
+++ b/solution.py
@@ -160,7 +160,17 @@
         lax.fori_loop(0, nvall // tile, columns, 0)
 
     def select(r, ybuf):
-        def orbital(g, carry):
+        def depart(d):
+            @pl.when(d > 0)
+            def _():
+                exchange(r, 0, d).start()
+
+            @pl.when(d == 0)
+            def _():
+                keep(r, 0).start()
+
+        def orbital(d, carry):
+            g = peer(q, d)
             dom = doms[pl.ds(g * OCC + r, 1), :]
             hot = []
             for n in range(nvall // tile):
@@ -173,13 +183,17 @@
             for b in range(rows // BLK):
                 m = mask_ref[b, g * OCC + r].astype(jnp.float32)
                 cbuf[r, b, g] = (acc[b * BLK:(b + 1) * BLK] * m).astype(jnp.bfloat16)
+
+            @pl.when(d > 0)
+            def _():
+                depart(d - 1)
             return carry
 
         lax.fori_loop(0, NQ, orbital, 0)
-        for h in range(2):
-            for d in range(1, NQ):
-                exchange(r, h, d).start()
-            keep(r, h).start()
+        depart(NQ - 1)
+        for d in range(1, NQ):
+            exchange(r, 1, d).start()
+        keep(r, 1).start()
 
     def send_on(r, h):
         keep(r, h).wait()

time: 205 us -> 203 us (level)
  the two profiles are of different devices: /device:TPU:7 before, /device:TPU:1 now
where the time goes in v4:
time: 203 us; the launch traced here: 200 us
  Pallas kernels  193 us (95%)
  local copies, waits for them, and re-layouts  6.54 us (3%)
    pallas_call x1, Pallas kernels, fused(): pl.pallas_call(fused_kernel, out_shape=(jax.ShapeDtypeStruct((NQ, OCC, ha...  191 us
    reshape x1, local copies, waits for them, and re-layouts, body(): return density.transpose(2, 3, 0, 1, 4).reshape(rows, local, nvir)  6.54 us

profile of v4, /device:TPU:1, one launch (start us, length us, event | category | flops | bytes accessed | tf_op | source)
XLA Modules:
  0.0 199.8 jit_solution(17630410820843658835)
XLA Ops:
  0.7 1.5 slot_table.1.slot_ref
  2.2 191.1 %pair_density.1 = (bf16[8,4,2,64,512]{4,3,2,1,0:T(8,128)(2,1)}, bf16[4,2,8,64,512]{4,3,2,1,0:T(8,128)(2,1)}) custom-call(s32[6,16]{1,0:T(8,128)} %slot_table.1.slot_ref, s32[2,32]{1,0:T(2,128)} %mask_ref.1, f32[512]{0:T(512)} %occ_ref.1, bf16[128,32,1024]{2,1,0:T(8,128)(2,1)} %x_ref.1, bf16[1024,2048]{1,0:T(8,128)(2,1)} %coef_ref.1, s32[512,512]{1,0:T(8,128)} %dom_ref.1, ...), custom_call_target="tpu_custom_call" | custom-call | tf_op jit(solution)/shard_map/pair_density/pallas_call | solution.py:415
  193.3 6.5 %copy.9 = bf16[128,32,512]{2,1,0:T(8,128)(2,1)} copy(bf16[128,32,512]{2,0,1:T(8,128)(2,1)} %bitcast.4) | data formatting | bytes 8388608 | tf_op jit(solution)/shard_map/reshape | solution.py:492
